TPU v7x, 256 devices: a whole 4x4x8 slice. The times are simulated.
256 devices in a mesh: unit: 16 (over x, z_lo), day: 16 (over y, z_hi, core).
Axes of the slice: x: 4, y: 4, z: 8 (z_hi: 2, z_lo: 4; z = z_hi * 4 + z_lo), core: 2. Of those that a mesh axis runs over, the one named last changes fastest.
Arguments:
- outcomes: float32 [65536, 4096], P('unit', 'day'), may hold values from -6 to 6
- cohort: int32 [65536], P('unit'), may hold values from 0 to 8
- pre_end: int32 [8], replicated, may hold values from 1024 to 2047
- post_start: int32 [8], replicated, may hold values from 2048 to 3071
- unit_logit: float32 [8, 65536], P(None, 'unit'), may hold values from -4 to 4
- time_logit: float32 [8, 4096], P(None, 'day'), may hold values from -4 to 4
Outputs:
- unit_weights: float32 [8, 65536], P(None, 'unit')
- time_weights: float32 [8, 4096], P(None, 'day')
All inputs are finite; a program needn't handle non-finite values.
Results may differ from a plain program's by a relative error of at most 0.0003.
Values sent between devices are 32-bit elements; how exact they have to be, the bound alone decides.
A program may use at most 64 MiB of HBM per device.

v0:
```python
import jax
import jax.numpy as jnp
from jax import lax
from jax.sharding import PartitionSpec as P

highest = lax.Precision.HIGHEST
step_rate = 16.0


def weigh_rows(left, outcomes):
    return jnp.dot(left, outcomes, precision=highest, preferred_element_type=jnp.float32)


def weigh_days(left, outcomes):
    return lax.dot_general(
        left,
        outcomes,
        (((1,), (1,)), ((), ())),
        precision=highest,
        preferred_element_type=jnp.float32,
    )


def local(outcomes, cohort, pre_end, post_start, unit_logit, time_logit):
    groups = pre_end.shape[0]
    unit_rows, day_cols = outcomes.shape
    day_devices = lax.axis_size("day")
    all_count = day_devices * day_cols
    labels = jnp.arange(groups, dtype=jnp.int32)[:, None]
    treated = (cohort[None, :] == labels).astype(jnp.float32)
    control = (cohort[None, :] > labels).astype(jnp.float32)
    day_start = lax.axis_index("day") * day_cols
    day_index = day_start + jnp.arange(day_cols, dtype=jnp.int32)[None, :]
    before = (day_index < pre_end[:, None]).astype(jnp.float32)
    before_len = pre_end.astype(jnp.float32)
    after_len = (all_count - post_start).astype(jnp.float32)
    raised = jnp.exp(unit_logit) * control
    unit_norm, treat_count, ctrl_count = lax.psum(
        (jnp.sum(raised, axis=1), jnp.sum(treated, axis=1), jnp.sum(control, axis=1)), "unit"
    )
    weights = raised / unit_norm[:, None]
    fitted, treat_sum = lax.psum(
        (weigh_rows(weights, outcomes), weigh_rows(treated, outcomes)), "unit"
    )
    residual = (fitted - treat_sum / jnp.maximum(treat_count, 1.0)[:, None]) * before
    ctrl_root = jnp.sqrt(jnp.maximum(ctrl_count, 1.0))[:, None]
    relaid = lax.all_to_all(outcomes, "day", split_axis=0, concat_axis=1, tiled=True)
    slab_rows = unit_rows // day_devices
    full_resid, full_logit = (
        lax.all_gather(residual, "day", axis=1, tiled=True),
        lax.all_gather(time_logit, "day", axis=1, tiled=True),
    )
    all_days = jnp.arange(all_count, dtype=jnp.int32)[None, :]
    full_before = (all_days < pre_end[:, None]).astype(jnp.float32)
    full_after = (all_days >= post_start[:, None]).astype(jnp.float32)
    row_start = lax.axis_index("day") * slab_rows
    sub_control = lax.dynamic_slice_in_dim(control, row_start, slab_rows, 1)
    sub_weights = lax.dynamic_slice_in_dim(weights, row_start, slab_rows, 1)
    unit_grad = weigh_days(full_resid, relaid)
    updated = sub_weights * jnp.exp(-step_rate * unit_grad / jnp.sqrt(before_len)[:, None])
    unit_total = lax.psum(jnp.sum(updated, axis=1), ("unit", "day"))
    row_share = updated / unit_total[:, None] * ctrl_count[:, None]
    unit_weights = lax.all_gather(row_share, "day", axis=1, tiled=True)
    time_raised = jnp.exp(full_logit) * full_before
    time_lam = time_raised / jnp.sum(time_raised, axis=1)[:, None]
    time_fit = weigh_days(time_lam, relaid)
    post_sum = weigh_days(full_after, relaid)
    shortfall = (time_fit - post_sum / after_len[:, None]) * sub_control
    time_grad = lax.psum(weigh_rows(shortfall, relaid), ("unit", "day"))
    moved = time_lam * jnp.exp(-step_rate * time_grad / ctrl_root)
    full_weights = moved / jnp.sum(moved, axis=1)[:, None] * before_len[:, None]
    time_weights = lax.dynamic_slice_in_dim(full_weights, day_start, day_cols, 1)
    return (unit_weights, time_weights)


def solution(mesh):
    return jax.shard_map(
        local,
        mesh=mesh,
        in_specs=(P("unit", "day"), P("unit"), P(), P(), P(None, "unit"), P(None, "day")),
        out_specs=(P(None, "unit"), P(None, "day")),
        check_vma=False,
    )
```

profile of v0, /device:TPU:2, one launch (start us, length us, event | category | flops | bytes accessed | tf_op | source)
XLA Modules:
  0.0 549.0 jit_solution(5261238960471951254)
XLA Ops:
  7.2 11.4 %all-to-all-start = ((f32[16,256,256]{2,1,0:T(8,128)}), f32[16,256,256]{2,1,0:T(8,128)}, u32[]{:S(2)}, u32[]{:S(2)}) async-start(f32[16,256,256]{2,1,0:T(8,128)} %bitcast.16), calls=%async_computation | async-start | bytes 8388608 | tf_op jit(solution)/shard_map/all_to_all | solution.py:47
  18.6 0.0 all-reduce.3.cloned.1.call-start
  18.7 0.2 fusion.13
  18.9 123.0 %psum.49 = f32[8]{0:T(128)S(1)} all-reduce(f32[8]{0:T(128)S(1)} %get-tuple-element.4), channel_id=1, replica_groups=mesh['unit'=16,'day'=16] {'unit'}, use_global_device_ids=true, to_apply=%region_1.0 | all-reduce | flops 8 | bytes 64 | tf_op jit(solution)/shard_map/psum | solution.py:38
  141.9 3.8 fusion.5
  145.7 0.1 fusion.7
  145.9 1.7 fusion.19
  147.6 73.4 %all-reduce = (f32[8,256]{1,0:T(8,128)S(1)}, f32[8,256]{1,0:T(8,128)S(1)}, f32[8]{0:T(128)S(1)}, f32[8]{0:T(128)S(1)}) all-reduce(f32[8,256]{1,0:T(8,128)S(1)} %fusion.19, f32[8,256]{1,0:T(8,128)S(1)} %fusion.5, f32[8]{0:T(128)S(1)} %get-tuple-element.3, f32[8]{0:T(128)S(1)} %get-tuple-element.2), channel_id=1, replica_groups=mesh['unit'=16,'day'=16] {'unit'}, use_global_device_ids=true, to_apply=%region_2.0 | all-reduce | flops 4112 | bytes 32896 | tf_op jit(solution)/shard_map/psum | solution.py:42
  221.0 29.0 %all_gather.11 = f32[8,4096]{1,0:T(8,128)S(1)} all-gather(f32[8,256]{1,0:T(8,128)S(1)} %copy-done.5), channel_id=1, replica_groups=mesh['unit'=16,'day'=16] {'day'}, dimensions={1}, use_global_device_ids=true | all-gather | bytes 139264 | tf_op jit(solution)/shard_map/all_gather | solution.py:51
  250.0 0.1 subtract_select_fusion
  250.0 25.6 %all_gather.9 = f32[8,4096]{1,0:T(8,128)S(1)} all-gather(f32[8,256]{1,0:T(8,128)S(1)} %subtract_select_fusion), channel_id=1, replica_groups=mesh['unit'=16,'day'=16] {'day'}, dimensions={1}, use_global_device_ids=true | all-gather | bytes 139264 | tf_op jit(solution)/shard_map/all_gather | solution.py:50
  275.7 0.2 fusion.10
  276.0 5.4 copy.8
  281.3 4.2 fusion.15
  285.5 1.5 fusion.1
  287.0 4.2 fusion.20
  291.2 4.0 fusion.18
  295.3 79.1 %psum.53 = f32[8]{0:T(128)S(1)} all-reduce(f32[8]{0:T(128)S(1)} %get-tuple-element.11), channel_id=1, replica_groups=mesh['unit'=16,'day'=16] {'unit','day'}, use_global_device_ids=true, to_apply=%region_7.0 | all-reduce | flops 8 | bytes 64 | tf_op jit(solution)/shard_map/psum | solution.py:61
  374.3 0.1 divide_multiply_fusion
  374.4 30.3 %all_gather.10 = f32[8,4096]{1,0:T(8,128)S(1)} all-gather(f32[8,256]{1,0:T(8,128)S(1)} %divide_multiply_fusion), channel_id=1, replica_groups=mesh['unit'=16,'day'=16] {'day'}, dimensions={1}, use_global_device_ids=true | all-gather | bytes 139264 | tf_op jit(solution)/shard_map/all_gather | solution.py:63
  404.7 135.0 %all-reduce.3.cloned.1.call-done = f32[8,4096]{1,0:T(8,128)} async-done(((f32[8,4096]{1,0:T(8,128)}), f32[8,4096]{1,0:T(8,128)}) %all-reduce.3.cloned.1.call-update) | async-done | bytes 131088 | tf_op jit(solution)/shard_map/psum | solution.py:69
  539.7 1.1 fusion.17
  540.8 0.7 fusion.14
  541.5 0.7 copy.11
  (23 shorter events, 0.1 us)
Async XLA Ops:
  7.2 11.5 %copy-start.2 = (f32[8,4096]{1,0:T(8,128)S(1)}, f32[8,4096]{1,0:T(8,128)}, u32[]{:S(2)}) copy-start(f32[8,4096]{1,0:T(8,128)} %param.10) | copy-start | bytes 393220
  7.2 11.5 %copy-start.3 = (s32[4096]{0:T(1024)S(1)}, s32[4096]{0:T(1024)}, u32[]{:S(2)}) copy-start(s32[4096]{0:T(1024)} %param.7) | copy-start | bytes 49156
  7.2 134.7 %copy-start.4 = (s32[8]{0:T(128)S(1)}, s32[8]{0:T(128)}, u32[]{:S(2)}) copy-start(s32[8]{0:T(128)} %param.8) | copy-start | bytes 100
  7.2 268.8 %all-to-all-start = ((f32[16,256,256]{2,1,0:T(8,128)}), f32[16,256,256]{2,1,0:T(8,128)}, u32[]{:S(2)}, u32[]{:S(2)}) async-start(f32[16,256,256]{2,1,0:T(8,128)} %bitcast.16), calls=%async_computation | async-start | bytes 8388608 | tf_op jit(solution)/shard_map/all_to_all | solution.py:47
  18.6 521.1 %all-reduce.3.cloned.1.call-start = ((), (), s32[]{:S(2)}) async-start(), calls=%async_computation.1 | async-start | bytes 262144 | tf_op jit(solution)/shard_map/psum | solution.py:69
  141.9 3.9 copy-start.1
  141.9 79.1 %copy-start.5 = (f32[8,256]{1,0:T(8,128)S(1)}, f32[8,256]{1,0:T(8,128)}, u32[]{:S(2)}) copy-start(f32[8,256]{1,0:T(8,128)} %param.11) | copy-start | bytes 24580
  141.9 134.0 %copy-start.6 = (s32[8]{0:T(128)S(1)}, s32[8]{0:T(128)}, u32[]{:S(2)}) copy-start(s32[8]{0:T(128)} %param.9) | copy-start | bytes 100
  281.3 4.2 copy-start
Sparse Core Ops, SparseCore 0:
  291.3 248.2 all-reduce.2
where the time goes:
time: 549 us
  blocking collectives  360 us (66%)
  waiting for transfers between devices  135 us (25%)
  matrix products  19.4 us (4%)
  between operations  14.2 us (3%)
  starting transfers between devices  11.4 us (2%)
  local copies, waits for them, and re-layouts  6.05 us (1%)
    psum x1, waiting for transfers between devices, local(): time_grad = lax.psum(weigh_rows(shortfall, relaid), ('unit', 'day'))  135 us
    psum x1, blocking collectives, local(): lax.psum((jnp.sum(raised, axis=1), jnp.sum(treated, axis=1), jnp.sum(cont...  123 us
    psum x1, blocking collectives, local(): unit_total = lax.psum(jnp.sum(updated, axis=1), ('unit', 'day'))  79.1 us
    psum x1, blocking collectives, local(): lax.psum((weigh_rows(weights, outcomes), weigh_rows(treated, outcomes)),...  73.4 us
    all_gather x1, blocking collectives, local(): unit_weights = lax.all_gather(row_share, 'day', axis=1, tiled=True)  30.3 us
    all_gather x1, blocking collectives, local(): lax.all_gather(time_logit, 'day', axis=1, tiled=True)  29 us
    all_gather x1, blocking collectives, local(): lax.all_gather(residual, 'day', axis=1, tiled=True)  25.6 us
    all_to_all x1, starting transfers between devices, local(): lax.all_to_all(outcomes, 'day', split_axis=0, concat_axis=1, tiled=True)  11.4 us
  transfers between devices with their start and end apart: 2, of which 1 were waited for; matrix products, arithmetic and copies ran while one was open for 2% of the time, Pallas kernels for 0%

commit v1 on v0

--- a/solution.py
+++ b/solution.py
@@ -58,7 +58,7 @@
     sub_weights = lax.dynamic_slice_in_dim(weights, row_start, slab_rows, 1)
     unit_grad = weigh_days(full_resid, relaid)
     updated = sub_weights * jnp.exp(-step_rate * unit_grad / jnp.sqrt(before_len)[:, None])
-    unit_total = lax.psum(jnp.sum(updated, axis=1), ("unit", "day"))
+    unit_total = lax.psum(lax.psum(jnp.sum(updated, axis=1), "day"), "unit")
     row_share = updated / unit_total[:, None] * ctrl_count[:, None]
     unit_weights = lax.all_gather(row_share, "day", axis=1, tiled=True)
     time_raised = jnp.exp(full_logit) * full_before

time: 549 us -> 597 us (1.087)
  waiting for transfers between devices: 135 us -> 182 us
    psum x1, waiting for transfers between devices: 135 us -> 182 us  [local(): time_grad = lax.psum(weigh_rows(shortfall, relaid), ('unit', 'day'))]
    psum x1 -> x2, blocking collectives: 123 us -> 161 us  [local(): lax.psum((jnp.sum(raised, axis=1), jnp.sum(treated, axis=1), jnp.sum(cont...]
    psum x1, blocking collectives: 79.1 us -> 47.7 us  [local(): unit_total = lax.psum(lax.psum(jnp.sum(updated, axis=1), 'day'), 'unit')]
    all_gather x1, blocking collectives: 30.3 us -> 24.3 us  [local(): unit_weights = lax.all_gather(row_share, 'day', axis=1, tiled=True)]
  transfers between devices with their start and end apart: 2 -> 2, of which waited for: 1 -> 1; matrix products, arithmetic and copies ran while one was open for 2% -> 1% of each run, Pallas kernels for 0% -> 0%
where the time goes in v1:
time: 597 us
  blocking collectives  361 us (60%)
  waiting for transfers between devices  182 us (30%)
  matrix products  19.4 us (3%)
  between operations  14.2 us (2%)
  starting transfers between devices  11.4 us (2%)
  local copies, waits for them, and re-layouts  6.04 us (1%)
    psum x1, waiting for transfers between devices, local(): time_grad = lax.psum(weigh_rows(shortfall, relaid), ('unit', 'day'))  182 us
    psum x2, blocking collectives, local(): lax.psum((jnp.sum(raised, axis=1), jnp.sum(treated, axis=1), jnp.sum(cont...  161 us
    psum x1, blocking collectives, local(): lax.psum((weigh_rows(weights, outcomes), weigh_rows(treated, outcomes)),...  73.4 us
    psum x1, blocking collectives, local(): unit_total = lax.psum(lax.psum(jnp.sum(updated, axis=1), 'day'), 'unit')  47.7 us
    all_gather x1, blocking collectives, local(): lax.all_gather(residual, 'day', axis=1, tiled=True)  29 us
    all_gather x1, blocking collectives, local(): lax.all_gather(time_logit, 'day', axis=1, tiled=True)  25.4 us
    all_gather x1, blocking collectives, local(): unit_weights = lax.all_gather(row_share, 'day', axis=1, tiled=True)  24.3 us
  transfers between devices with their start and end apart: 2, of which 1 were waited for; matrix products, arithmetic and copies ran while one was open for 1% of the time, Pallas kernels for 0%

profile of v1, /device:TPU:2, one launch (start us, length us, event | category | flops | bytes accessed | tf_op | source)
XLA Modules:
  0.0 596.5 jit_solution(6766060188058199070)
XLA Ops:
  7.2 11.4 %all-to-all-start = ((f32[16,256,256]{2,1,0:T(8,128)}), f32[16,256,256]{2,1,0:T(8,128)}, u32[]{:S(2)}, u32[]{:S(2)}) async-start(f32[16,256,256]{2,1,0:T(8,128)} %bitcast.16), calls=%async_computation | async-start | bytes 8388608 | tf_op jit(solution)/shard_map/all_to_all | solution.py:47
  18.7 0.2 fusion.13
  18.9 123.0 %psum.56 = f32[8]{0:T(128)S(1)} all-reduce(f32[8]{0:T(128)S(1)} %get-tuple-element.4), channel_id=1, replica_groups=mesh['unit'=16,'day'=16] {'unit'}, use_global_device_ids=true, to_apply=%region_1.0 | all-reduce | flops 8 | bytes 64 | tf_op jit(solution)/shard_map/psum | solution.py:38
  141.9 3.8 fusion.5
  145.7 0.1 fusion.7
  145.9 1.7 fusion.19
  147.6 73.4 %all-reduce.1 = (f32[8,256]{1,0:T(8,128)S(1)}, f32[8,256]{1,0:T(8,128)S(1)}, f32[8]{0:T(128)S(1)}) all-reduce(f32[8,256]{1,0:T(8,128)S(1)} %fusion.19, f32[8,256]{1,0:T(8,128)S(1)} %fusion.5, f32[8]{0:T(128)S(1)} %get-tuple-element.3), channel_id=1, replica_groups=mesh['unit'=16,'day'=16] {'unit'}, use_global_device_ids=true, to_apply=%region_2.0 | all-reduce | flops 4104 | bytes 32832 | tf_op jit(solution)/shard_map/psum | solution.py:42
  221.0 0.1 subtract_select_fusion
  221.1 29.0 %all_gather.9 = f32[8,4096]{1,0:T(8,128)S(1)} all-gather(f32[8,256]{1,0:T(8,128)S(1)} %subtract_select_fusion), channel_id=1, replica_groups=mesh['unit'=16,'day'=16] {'day'}, dimensions={1}, use_global_device_ids=true | all-gather | bytes 139264 | tf_op jit(solution)/shard_map/all_gather | solution.py:50
  250.0 25.4 %all_gather.11 = f32[8,4096]{1,0:T(8,128)S(1)} all-gather(f32[8,256]{1,0:T(8,128)S(1)} %copy-done.5), channel_id=1, replica_groups=mesh['unit'=16,'day'=16] {'day'}, dimensions={1}, use_global_device_ids=true | all-gather | bytes 139264 | tf_op jit(solution)/shard_map/all_gather | solution.py:51
  275.5 0.2 fusion.10
  275.8 5.4 copy.8
  281.1 4.0 fusion.18
  285.2 47.7 %psum.60 = f32[8]{0:T(128)S(1)} all-reduce(f32[8]{0:T(128)S(1)} %get-tuple-element.12), channel_id=1, replica_groups=mesh['unit'=16,'day'=16] {'day'}, use_global_device_ids=true, to_apply=%region_7.0 | all-reduce | flops 8 | bytes 64 | tf_op jit(solution)/shard_map/psum | solution.py:61
  332.9 4.2 fusion.15
  337.1 1.5 fusion.1
  338.5 4.2 fusion.20
  342.8 38.0 %all-reduce = (f32[8]{0:T(128)S(1)}, f32[8]{0:T(128)S(1)}) all-reduce(f32[8]{0:T(128)S(1)} %get-tuple-element.2, f32[8]{0:T(128)S(1)} %psum.60), channel_id=1, replica_groups=mesh['unit'=16,'day'=16] {'unit'}, use_global_device_ids=true, to_apply=%region_10.0 | all-reduce | flops 16 | bytes 128 | tf_op jit(solution)/shard_map/psum | solution.py:38
  380.8 0.1 divide_multiply_fusion
  380.9 24.3 %all_gather.10 = f32[8,4096]{1,0:T(8,128)S(1)} all-gather(f32[8,256]{1,0:T(8,128)S(1)} %divide_multiply_fusion), channel_id=1, replica_groups=mesh['unit'=16,'day'=16] {'day'}, dimensions={1}, use_global_device_ids=true | all-gather | bytes 139264 | tf_op jit(solution)/shard_map/all_gather | solution.py:63
  405.2 182.0 %all-reduce.4.cloned.1.call-done = f32[8,4096]{1,0:T(8,128)} async-done(((f32[8,4096]{1,0:T(8,128)}), f32[8,4096]{1,0:T(8,128)}) %all-reduce.4.cloned.1.call-update) | async-done | bytes 131088 | tf_op jit(solution)/shard_map/psum | solution.py:69
  587.2 1.1 fusion.17
  588.3 0.7 fusion.14
  589.0 0.7 copy.11
  (24 shorter events, 0.1 us)
Async XLA Ops:
  7.2 11.5 %copy-start.2 = (f32[8,4096]{1,0:T(8,128)S(1)}, f32[8,4096]{1,0:T(8,128)}, u32[]{:S(2)}) copy-start(f32[8,4096]{1,0:T(8,128)} %param.10) | copy-start | bytes 393220
  7.2 11.5 %copy-start.3 = (s32[4096]{0:T(1024)S(1)}, s32[4096]{0:T(1024)}, u32[]{:S(2)}) copy-start(s32[4096]{0:T(1024)} %param.7) | copy-start | bytes 49156
  7.2 134.7 %copy-start.4 = (s32[8]{0:T(128)S(1)}, s32[8]{0:T(128)}, u32[]{:S(2)}) copy-start(s32[8]{0:T(128)} %param.8) | copy-start | bytes 100
  7.2 268.6 %all-to-all-start = ((f32[16,256,256]{2,1,0:T(8,128)}), f32[16,256,256]{2,1,0:T(8,128)}, u32[]{:S(2)}, u32[]{:S(2)}) async-start(f32[16,256,256]{2,1,0:T(8,128)} %bitcast.16), calls=%async_computation | async-start | bytes 8388608 | tf_op jit(solution)/shard_map/all_to_all | solution.py:47
  18.6 568.6 %all-reduce.4.cloned.1.call-start = ((), (), s32[]{:S(2)}) async-start(), calls=%async_computation.1 | async-start | bytes 262144 | tf_op jit(solution)/shard_map/psum | solution.py:69
  141.9 3.9 copy-start.1
  141.9 108.1 %copy-start.5 = (f32[8,256]{1,0:T(8,128)S(1)}, f32[8,256]{1,0:T(8,128)}, u32[]{:S(2)}) copy-start(f32[8,256]{1,0:T(8,128)} %param.11) | copy-start | bytes 24580
  141.9 133.8 %copy-start.6 = (s32[8]{0:T(128)S(1)}, s32[8]{0:T(128)}, u32[]{:S(2)}) copy-start(s32[8]{0:T(128)} %param.9) | copy-start | bytes 100
  332.9 4.2 copy-start
Sparse Core Ops, SparseCore 0:
  342.9 244.2 all-reduce.3

commit v2 on v0

--- a/solution.py
+++ b/solution.py
@@ -66,7 +66,7 @@
     time_fit = weigh_days(time_lam, relaid)
     post_sum = weigh_days(full_after, relaid)
     shortfall = (time_fit - post_sum / after_len[:, None]) * sub_control
-    time_grad = lax.psum(weigh_rows(shortfall, relaid), ("unit", "day"))
+    time_grad = lax.psum(lax.psum(weigh_rows(shortfall, relaid), "unit"), "day")
     moved = time_lam * jnp.exp(-step_rate * time_grad / ctrl_root)
     full_weights = moved / jnp.sum(moved, axis=1)[:, None] * before_len[:, None]
     time_weights = lax.dynamic_slice_in_dim(full_weights, day_start, day_cols, 1)

time: 549 us -> 644 us (1.17)
  waiting for transfers between devices: 135 us -> 227 us
    psum x1 -> x2, waiting for transfers between devices: 135 us -> 227 us  [local(): time_grad = lax.psum(lax.psum(weigh_rows(shortfall, relaid), 'unit'), 'day')]
  transfers between devices with their start and end apart: 2 -> 3, of which waited for: 1 -> 2; matrix products, arithmetic and copies ran while one was open for 2% -> 2% of each run, Pallas kernels for 0% -> 0%
where the time goes in v2:
time: 644 us; the launch traced here: 642 us
  blocking collectives  362 us (56%)
  waiting for transfers between devices  227 us (35%)
  matrix products  19.4 us (3%)
  between operations  14.2 us (2%)
  starting transfers between devices  11.7 us (2%)
    psum x2, waiting for transfers between devices, local(): time_grad = lax.psum(lax.psum(weigh_rows(shortfall, relaid), 'unit'), 'day')  227 us
    psum x1, blocking collectives, local(): lax.psum((jnp.sum(raised, axis=1), jnp.sum(treated, axis=1), jnp.sum(cont...  123 us
    psum x1, blocking collectives, local(): unit_total = lax.psum(jnp.sum(updated, axis=1), ('unit', 'day'))  79.4 us
    psum x1, blocking collectives, local(): lax.psum((weigh_rows(weights, outcomes), weigh_rows(treated, outcomes)),...  73.4 us
    all_gather x1, blocking collectives, local(): unit_weights = lax.all_gather(row_share, 'day', axis=1, tiled=True)  31.4 us
    all_gather x1, blocking collectives, local(): lax.all_gather(time_logit, 'day', axis=1, tiled=True)  29 us
    all_gather x1, blocking collectives, local(): lax.all_gather(residual, 'day', axis=1, tiled=True)  25.5 us
  transfers between devices with their start and end apart: 3, of which 2 were waited for; matrix products, arithmetic and copies ran while one was open for 2% of the time, Pallas kernels for 0%

profile of v2, /device:TPU:2, one launch (start us, length us, event | category | flops | bytes accessed | tf_op | source)
XLA Modules:
  0.0 642.2 jit_solution(14951598003741277257)
XLA Ops:
  7.2 11.4 %all-to-all-start = ((f32[16,256,256]{2,1,0:T(8,128)}), f32[16,256,256]{2,1,0:T(8,128)}, u32[]{:S(2)}, u32[]{:S(2)}) async-start(f32[16,256,256]{2,1,0:T(8,128)} %bitcast.16), calls=%async_computation | async-start | bytes 8388608 | tf_op jit(solution)/shard_map/all_to_all | solution.py:47
  18.7 0.2 fusion.13
  18.9 123.0 %psum.56 = f32[8]{0:T(128)S(1)} all-reduce(f32[8]{0:T(128)S(1)} %get-tuple-element.4), channel_id=1, replica_groups=mesh['unit'=16,'day'=16] {'unit'}, use_global_device_ids=true, to_apply=%region_1.0 | all-reduce | flops 8 | bytes 64 | tf_op jit(solution)/shard_map/psum | solution.py:38
  141.9 3.8 fusion.5
  145.7 0.1 fusion.7
  145.9 1.7 fusion.19
  147.6 73.4 %all-reduce = (f32[8,256]{1,0:T(8,128)S(1)}, f32[8,256]{1,0:T(8,128)S(1)}, f32[8]{0:T(128)S(1)}, f32[8]{0:T(128)S(1)}) all-reduce(f32[8,256]{1,0:T(8,128)S(1)} %fusion.19, f32[8,256]{1,0:T(8,128)S(1)} %fusion.5, f32[8]{0:T(128)S(1)} %get-tuple-element.3, f32[8]{0:T(128)S(1)} %get-tuple-element.2), channel_id=1, replica_groups=mesh['unit'=16,'day'=16] {'unit'}, use_global_device_ids=true, to_apply=%region_2.0 | all-reduce | flops 4112 | bytes 32896 | tf_op jit(solution)/shard_map/psum | solution.py:42
  221.0 29.0 %all_gather.11 = f32[8,4096]{1,0:T(8,128)S(1)} all-gather(f32[8,256]{1,0:T(8,128)S(1)} %copy-done.5), channel_id=1, replica_groups=mesh['unit'=16,'day'=16] {'day'}, dimensions={1}, use_global_device_ids=true | all-gather | bytes 139264 | tf_op jit(solution)/shard_map/all_gather | solution.py:51
  250.0 0.1 subtract_select_fusion
  250.0 25.5 %all_gather.9 = f32[8,4096]{1,0:T(8,128)S(1)} all-gather(f32[8,256]{1,0:T(8,128)S(1)} %subtract_select_fusion), channel_id=1, replica_groups=mesh['unit'=16,'day'=16] {'day'}, dimensions={1}, use_global_device_ids=true | all-gather | bytes 139264 | tf_op jit(solution)/shard_map/all_gather | solution.py:50
  275.5 0.2 fusion.10
  275.8 5.4 copy.8
  281.1 4.2 fusion.15
  285.3 1.5 fusion.1
  286.8 4.2 fusion.20
  291.0 0.2 all-reduce.6.cloned.1.call-start
  291.3 4.0 fusion.18
  295.3 79.4 %psum.60 = f32[8]{0:T(128)S(1)} all-reduce(f32[8]{0:T(128)S(1)} %get-tuple-element.11), channel_id=1, replica_groups=mesh['unit'=16,'day'=16] {'unit','day'}, use_global_device_ids=true, to_apply=%region_7.0 | all-reduce | flops 8 | bytes 64 | tf_op jit(solution)/shard_map/psum | solution.py:61
  374.7 74.0 %all-reduce.4.cloned.1.call-done = f32[8,4096]{1,0:T(8,128)} async-done(((f32[8,4096]{1,0:T(8,128)}), f32[8,4096]{1,0:T(8,128)}) %all-reduce.4.cloned.1.call-update) | async-done | bytes 131088 | tf_op jit(solution)/shard_map/psum | solution.py:69
  448.9 31.4 %all_gather.10 = f32[8,4096]{1,0:T(8,128)S(1)} all-gather(f32[8,256]{1,0:T(8,128)S(1)} %divide_multiply_fusion), channel_id=1, replica_groups=mesh['unit'=16,'day'=16] {'day'}, dimensions={1}, use_global_device_ids=true | all-gather | bytes 139264 | tf_op jit(solution)/shard_map/all_gather | solution.py:63
  480.2 152.7 %all-reduce.6.cloned.1.call-done = f32[8,4096]{1,0:T(8,128)} async-done(((f32[8,4096]{1,0:T(8,128)}), f32[8,4096]{1,0:T(8,128)}) %all-reduce.6.cloned.1.call-update) | async-done | bytes 131088 | tf_op jit(solution)/shard_map/psum | solution.py:69
  632.9 1.1 fusion.17
  634.0 0.7 fusion.14
  634.7 0.7 copy.12
  (26 shorter events, 0.2 us)
Async XLA Ops:
  7.2 11.5 %copy-start.2 = (f32[8,4096]{1,0:T(8,128)S(1)}, f32[8,4096]{1,0:T(8,128)}, u32[]{:S(2)}) copy-start(f32[8,4096]{1,0:T(8,128)} %param.10) | copy-start | bytes 393220
  7.2 11.5 %copy-start.3 = (s32[4096]{0:T(1024)S(1)}, s32[4096]{0:T(1024)}, u32[]{:S(2)}) copy-start(s32[4096]{0:T(1024)} %param.7) | copy-start | bytes 49156
  7.2 134.7 %copy-start.4 = (s32[8]{0:T(128)S(1)}, s32[8]{0:T(128)}, u32[]{:S(2)}) copy-start(s32[8]{0:T(128)} %param.8) | copy-start | bytes 100
  7.2 268.6 %all-to-all-start = ((f32[16,256,256]{2,1,0:T(8,128)}), f32[16,256,256]{2,1,0:T(8,128)}, u32[]{:S(2)}, u32[]{:S(2)}) async-start(f32[16,256,256]{2,1,0:T(8,128)} %bitcast.16), calls=%async_computation | async-start | bytes 8388608 | tf_op jit(solution)/shard_map/all_to_all | solution.py:47
  18.6 430.2 %all-reduce.4.cloned.1.call-start = ((), (), s32[]{:S(2)}) async-start(), calls=%async_computation.1 | async-start | bytes 262144 | tf_op jit(solution)/shard_map/psum | solution.py:69
  141.9 3.9 copy-start.1
  141.9 79.1 %copy-start.5 = (f32[8,256]{1,0:T(8,128)S(1)}, f32[8,256]{1,0:T(8,128)}, u32[]{:S(2)}) copy-start(f32[8,256]{1,0:T(8,128)} %param.11) | copy-start | bytes 24580
  141.9 133.8 %copy-start.6 = (s32[8]{0:T(128)S(1)}, s32[8]{0:T(128)}, u32[]{:S(2)}) copy-start(s32[8]{0:T(128)} %param.9) | copy-start | bytes 100
  281.1 4.2 copy-start
  291.0 341.9 %all-reduce.6.cloned.1.call-start = ((), (), s32[]{:S(2)}) async-start(), calls=%async_computation.2 | async-start | bytes 262144 | tf_op jit(solution)/shard_map/psum | solution.py:69
Sparse Core Ops, SparseCore 0:
  291.1 157.5 all-reduce.3
  451.4 181.4 all-reduce.5
